TPU v7x, 32 devices: a whole 2x2x4 slice. The times are simulated.
32 devices in a mesh: fsdp: 8 (over y, x, core), ep: 4 (over z).
Axes of the slice: x: 2, y: 2, z: 4, core: 2. Of those that a mesh axis runs over, the one named last changes fastest.
Arguments:
- hidden: bfloat16 [2048, 8192], P('fsdp', 'ep'), may hold values from -6 to 6
- w_down: bfloat16 [6144, 2, 8192], P('fsdp', None, 'ep'), may hold values from -0.0625 to 0.0625
- route_ids: int32 [1024, 2], P('fsdp'), may hold values from 0 to 7, as said below
- probs: float32 [1024, 2], P('fsdp'), may hold values from 0.1 to 0.9
- grad_out: bfloat16 [1024, 6144], P('fsdp', 'ep'), may hold values from -6 to 6
Outputs:
- output: bfloat16 [1024, 6144], P('fsdp', 'ep')
- grad_hidden: bfloat16 [2048, 8192], P('fsdp', 'ep')
- grad_weight: bfloat16 [6144, 2, 8192], P('fsdp', None, 'ep')
- grad_probs: float32 [1024, 2], P('fsdp')
Inputs may be any that keep to these rules, and one draw needn't show every extreme that they name: `route_ids`: each token names 2 different experts. Within one panel's 128 tokens, experts 0 and 1 are each named by 1 to 128 tokens, and in some panel both are named by all 128 tokens.
All inputs are finite; a program needn't handle non-finite values.
Results may differ from a plain program's by a relative error of at most 0.012.
Values may be sent and summed in bfloat16 or wider, within the bound.
A program may use at most 384 MiB of HBM per device.

v0:
```python
import jax
import jax.numpy as jnp
from jax import lax
from jax.sharding import PartitionSpec as P

BLOCK = 128


def route_layout(route_part, prob_part, expert_count, block_rows, row_count):
    token_count = route_part.shape[0]
    experts = jnp.arange(expert_count, dtype=jnp.int32)
    hits = (route_part[:, :, None] == experts[None, None, :]).astype(jnp.int32)
    named = jnp.sum(hits, axis=1)
    counts = jnp.sum(named, axis=0)
    ranks = jnp.cumsum(named, axis=0) - named
    padded = (counts + block_rows - 1) // block_rows * block_rows
    offsets = jnp.cumsum(padded) - padded
    row_of = jnp.sum(hits * (offsets[None, None, :] + ranks[:, None, :]), axis=2)
    valid = jnp.sum(hits, axis=2)
    starts = jnp.arange(row_count // block_rows, dtype=jnp.int32) * block_rows
    inside = (starts[:, None] >= offsets[None, :]) & (starts[:, None] < (offsets + padded)[None, :])
    block_exp = jnp.sum(jnp.where(inside, experts[None, :] + 1, 0), axis=1) - 1
    target = jnp.where(valid > 0, row_of, row_count).reshape(-1)
    token_index = jnp.broadcast_to(
        jnp.arange(token_count, dtype=jnp.int32)[:, None], route_part.shape
    ).reshape(-1)
    row_tok = jnp.zeros((row_count,), jnp.int32).at[target].set(token_index, mode="drop")
    row_live = (
        jnp.zeros((row_count,), jnp.int32).at[target].set(jnp.ones_like(token_index), mode="drop")
    )
    row_prob = (
        jnp.zeros((row_count,), prob_part.dtype).at[target].set(prob_part.reshape(-1), mode="drop")
    )
    return (row_of, valid, block_exp, row_tok, row_live, row_prob)


def local(hidden, w_down, route_ids, probs, grad_out):
    row_count, unit_count = hidden.shape
    expert_count = w_down.shape[1]
    block_count = row_count // BLOCK
    row_of, valid, block_exp, row_tok, row_live, row_prob = route_layout(
        route_ids, probs, expert_count, BLOCK, row_count
    )
    safe_exp = jnp.maximum(block_exp, 0)
    prob_valid = probs * valid.astype(jnp.float32)
    full_grads = lax.all_gather(grad_out, "ep", axis=1, tiled=True)
    model_width = full_grads.shape[1]
    routed = jnp.where(row_live[:, None] > 0, full_grads[row_tok], jnp.zeros((), jnp.bfloat16))
    scaled = (row_prob[:, None] * routed.astype(jnp.float32)).astype(jnp.bfloat16)
    hid_blocks = hidden.reshape(block_count, BLOCK, unit_count)
    routed_blocks = routed.reshape(block_count, BLOCK, model_width)
    row_exp = jnp.repeat(block_exp, BLOCK)
    member = (row_exp[:, None] == jnp.arange(expert_count, dtype=jnp.int32)[None, :]).astype(
        jnp.bfloat16
    )
    masked_hid = hidden[:, None, :] * member[:, :, None]
    piece = lax.all_gather(w_down, "fsdp", axis=0, tiled=True)
    width = piece.shape[0]
    chosen = jnp.take(piece, safe_exp, axis=1)
    out_rows = jnp.einsum(
        "bri,dbi->brd", hid_blocks, chosen, preferred_element_type=jnp.float32
    ).reshape(row_count, width)
    back_total = jnp.einsum(
        "brd,dbi->bri", routed_blocks, chosen, preferred_element_type=jnp.float32
    )
    combined = jnp.sum(prob_valid[:, :, None] * out_rows[row_of], axis=1)
    out_total = combined
    out_total, back_total = (out_total, back_total)
    grad_weight = lax.psum_scatter(
        jnp.einsum("rd,rei->dei", scaled, masked_hid, preferred_element_type=jnp.float32).astype(
            jnp.bfloat16
        ),
        "fsdp",
        scatter_dimension=0,
        tiled=True,
    )
    output = lax.psum_scatter(out_total.astype(jnp.bfloat16), "ep", scatter_dimension=1, tiled=True)
    hidden_back = back_total.reshape(row_count, unit_count)
    grad_hidden = (row_prob[:, None] * hidden_back).astype(jnp.bfloat16)
    row_dot = jnp.sum(hidden.astype(jnp.float32) * hidden_back, axis=1)
    prob_terms = valid.astype(jnp.float32) * row_dot[row_of]
    grad_probs = lax.psum(prob_terms, "ep")
    return (output, grad_hidden, grad_weight, grad_probs)


def solution(mesh):
    placed = (
        P("fsdp", "ep"),
        P("fsdp", None, "ep"),
        P("fsdp", None),
        P("fsdp", None),
        P("fsdp", "ep"),
    )
    return jax.shard_map(
        local,
        mesh=mesh,
        in_specs=placed,
        out_specs=(P("fsdp", "ep"), P("fsdp", "ep"), P("fsdp", None, "ep"), P("fsdp", None)),
        check_vma=False,
    )
```

profile of v0, /device:TPU:0, one launch (start us, length us, event | category | flops | bytes accessed | tf_op | source)
XLA Modules:
  0.0 635.5 jit_solution(14992355778642910269)
XLA Ops:
  7.9 8.4 %copy.21 = bf16[768,2,2048]{2,0,1:T(8,128)(2,1)} copy(bf16[768,2,2048]{2,1,0:T(2,128)(2,1)} %param.6) | data formatting | bytes 12582912 | tf_op args[1]
  23.5 25.9 %all-gather.5.cloned.1.call-done = bf16[128,6144]{1,0:T(8,128)(2,1)} async-done(((bf16[128,1536]{1,0:T(8,128)(2,1)}), bf16[128,6144]{1,0:T(8,128)(2,1)}) %all-gather.5.cloned.1.call-update) | async-done | bytes 1572880 | tf_op jit(solution)/shard_map/all_gather | solution.py:46
  49.4 7.1 %gather_fusion.1 = bf16[256,6144]{1,0:T(8,128)(2,1)S(1)} fusion(bf16[128,6144]{1,0:T(8,128)(2,1)} %all-gather.5.cloned.1.call-done, s32[1024]{0:T(1024)S(1)} %pad_clamp_fusion), kind=kCustom, calls=%fused_computation.1 | custom fusion | bytes 6292480 | tf_op jit(solution)/shard_map/gather | solution.py:48
  56.5 24.9 %convolution_convert_fusion = bf16[6144,2,2048]{2,0,1:T(8,128)(2,1)} fusion(bf16[256,6144]{1,0:T(8,128)(2,1)S(1)} %gather_fusion.1, f32[256]{0:T(256)S(1)} %scatter_custom_fusion, pred[256]{0:T(512)(128)(4,1)S(1)} %broadcast_compare_fusion, bf16[256,2]{0,1:T(2,128)(2,1)S(1)} %compare_convert_fusion, bf16[256,2048]{1,0:T(8,128)(2,1)} %param.5), kind=kOutput, calls=%fused_computation.31 | convolution fusion | flops 12920553472 | bytes 54528256 | tf_op jit(solution)/shard_map/rd,rei->dei/dot_general | solution.py:70
  83.2 199.5 %all-gather.3.cloned.1.call-done = bf16[6144,2,2048]{2,0,1:T(8,128)(2,1)} async-done(((bf16[768,2,2048]{2,0,1:T(8,128)(2,1)}), bf16[6144,2,2048]{2,0,1:T(8,128)(2,1)}) %all-gather.3.cloned.1.call-update) | async-done | bytes 50331664 | tf_op jit(solution)/shard_map/all_gather | solution.py:57
  282.7 41.5 %fusion.28 = (bf16[512,2,2048]{2,0,1:T(8,128)(2,1)}, bf16[512,2,2048]{2,0,1:T(8,128)(2,1)}, bf16[512,2,2048]{2,0,1:T(8,128)(2,1)}, bf16[512,2,2048]{2,0,1:T(8,12...) fusion(bf16[6144,2,2048]{2,0,1:T(8,128)(2,1)} %all-gather.3.clo, ...), kind=kLoop, calls=%fused_computation.108 | loop fusion | bytes 100663296 | tf_op jit(solution)/shard_map/jit(_take)/gather | solution.py:59
  327.2 9.6 %while.12 = (s32[]{:T(128)}, bf16[512,2,2048]{2,0,1:T(8,128)(2,1)}, s32[2,1]{0,1:T(1,128)S(1)}, bf16[2,512,2048]{2,1,0:T(8,128)(2,1)}, s32[]{:T(128)}) while((s32[]{:T(128)}, bf16[512,2,2048]{2,0,1:T(8,128)(2,1)}, s32[2,1]{0,1:T(1,128)S(1)}, bf16[2,512,2048]{2,1,0:T(8,128)(2,1)}, s32[]{:T(128)}) %tuple.161), condition=%wide.while_cond, body=%wide.while_body.sunk | while | flops 2 | bytes 4195401 | solution.py:59
  327.8 4.2 bitcast_dynamic-update-slice_fusion.36
  332.5 4.3 bitcast_dynamic-update-slice_fusion.36
  339.9 9.5 %while.13 = (s32[]{:T(128)}, bf16[512,2,2048]{2,0,1:T(8,128)(2,1)}, s32[2,1]{0,1:T(1,128)S(1)}, bf16[2,512,2048]{2,1,0:T(8,128)(2,1)}, s32[]{:T(128)}) while((s32[]{:T(128)}, bf16[512,2,2048]{2,0,1:T(8,128)(2,1)}, s32[2,1]{0,1:T(1,128)S(1)}, bf16[2,512,2048]{2,1,0:T(8,128)(2,1)}, s32[]{:T(128)}) %tuple.205), condition=%wide.while_cond.1, body=%wide.while_body.1.sunk | while | flops 2 | bytes 4195401 | solution.py:59
  340.5 4.3 bitcast_dynamic-update-slice_fusion.37
  345.4 4.0 bitcast_dynamic-update-slice_fusion.37
  352.0 8.8 %while.14 = (s32[]{:T(128)}, bf16[512,2,2048]{2,0,1:T(8,128)(2,1)}, s32[2,1]{0,1:T(1,128)S(1)}, bf16[2,512,2048]{2,1,0:T(8,128)(2,1)}, s32[]{:T(128)}) while((s32[]{:T(128)}, bf16[512,2,2048]{2,0,1:T(8,128)(2,1)}, s32[2,1]{0,1:T(1,128)S(1)}, bf16[2,512,2048]{2,1,0:T(8,128)(2,1)}, s32[]{:T(128)}) %tuple.206), condition=%wide.while_cond.2, body=%wide.while_body.2.sunk | while | flops 2 | bytes 4195401 | solution.py:59
  352.5 3.8 bitcast_dynamic-update-slice_fusion.38
  356.9 3.9 bitcast_dynamic-update-slice_fusion.38
  363.4 9.2 %while.15 = (s32[]{:T(128)}, bf16[512,2,2048]{2,0,1:T(8,128)(2,1)}, s32[2,1]{0,1:T(1,128)S(1)}, bf16[2,512,2048]{2,1,0:T(8,128)(2,1)}, s32[]{:T(128)}) while((s32[]{:T(128)}, bf16[512,2,2048]{2,0,1:T(8,128)(2,1)}, s32[2,1]{0,1:T(1,128)S(1)}, bf16[2,512,2048]{2,1,0:T(8,128)(2,1)}, s32[]{:T(128)}) %tuple.207), condition=%wide.while_cond.3, body=%wide.while_body.3.sunk | while | flops 2 | bytes 4195401 | solution.py:59
  363.9 4.1 bitcast_dynamic-update-slice_fusion.39
  368.6 3.9 bitcast_dynamic-update-slice_fusion.39
  375.1 9.1 %while.16 = (s32[]{:T(128)}, bf16[512,2,2048]{2,0,1:T(8,128)(2,1)}, s32[2,1]{0,1:T(1,128)S(1)}, bf16[2,512,2048]{2,1,0:T(8,128)(2,1)}, s32[]{:T(128)}) while((s32[]{:T(128)}, bf16[512,2,2048]{2,0,1:T(8,128)(2,1)}, s32[2,1]{0,1:T(1,128)S(1)}, bf16[2,512,2048]{2,1,0:T(8,128)(2,1)}, s32[]{:T(128)}) %tuple.208), condition=%wide.while_cond.4, body=%wide.while_body.4.sunk | while | flops 2 | bytes 4195401 | solution.py:59
  375.7 3.9 bitcast_dynamic-update-slice_fusion.40
  380.1 4.1 bitcast_dynamic-update-slice_fusion.40
  386.7 8.8 %while.17 = (s32[]{:T(128)}, bf16[512,2,2048]{2,0,1:T(8,128)(2,1)}, s32[2,1]{0,1:T(1,128)S(1)}, bf16[2,512,2048]{2,1,0:T(8,128)(2,1)}, s32[]{:T(128)}) while((s32[]{:T(128)}, bf16[512,2,2048]{2,0,1:T(8,128)(2,1)}, s32[2,1]{0,1:T(1,128)S(1)}, bf16[2,512,2048]{2,1,0:T(8,128)(2,1)}, s32[]{:T(128)}) %tuple.209), condition=%wide.while_cond.5, body=%wide.while_body.5.sunk | while | flops 2 | bytes 4195401 | solution.py:59
  391.6 3.8 bitcast_dynamic-update-slice_fusion.41
  398.1 8.8 %while.18 = (s32[]{:T(128)}, bf16[512,2,2048]{2,0,1:T(8,128)(2,1)}, s32[2,1]{0,1:T(1,128)S(1)}, bf16[2,512,2048]{2,1,0:T(8,128)(2,1)}, s32[]{:T(128)}) while((s32[]{:T(128)}, bf16[512,2,2048]{2,0,1:T(8,128)(2,1)}, s32[2,1]{0,1:T(1,128)S(1)}, bf16[2,512,2048]{2,1,0:T(8,128)(2,1)}, s32[]{:T(128)}) %tuple.210), condition=%wide.while_cond.6, body=%wide.while_body.6.sunk | while | flops 2 | bytes 4195401 | solution.py:59
  398.6 3.8 bitcast_dynamic-update-slice_fusion.42
  403.0 3.9 bitcast_dynamic-update-slice_fusion.42
  409.4 9.3 %while.19 = (s32[]{:T(128)}, bf16[512,2,2048]{2,0,1:T(8,128)(2,1)}, s32[2,1]{0,1:T(1,128)S(1)}, bf16[2,512,2048]{2,1,0:T(8,128)(2,1)}, s32[]{:T(128)}) while((s32[]{:T(128)}, bf16[512,2,2048]{2,0,1:T(8,128)(2,1)}, s32[2,1]{0,1:T(1,128)S(1)}, bf16[2,512,2048]{2,1,0:T(8,128)(2,1)}, s32[]{:T(128)}) %tuple.211), condition=%wide.while_cond.7, body=%wide.while_body.7.sunk | while | flops 2 | bytes 4195401 | solution.py:59
  410.0 4.2 bitcast_dynamic-update-slice_fusion.43
  414.8 4.0 bitcast_dynamic-update-slice_fusion.43
  421.2 8.8 %while.20 = (s32[]{:T(128)}, bf16[512,2,2048]{2,0,1:T(8,128)(2,1)}, s32[2,1]{0,1:T(1,128)S(1)}, bf16[2,512,2048]{2,1,0:T(8,128)(2,1)}, s32[]{:T(128)}) while((s32[]{:T(128)}, bf16[512,2,2048]{2,0,1:T(8,128)(2,1)}, s32[2,1]{0,1:T(1,128)S(1)}, bf16[2,512,2048]{2,1,0:T(8,128)(2,1)}, s32[]{:T(128)}) %tuple.212), condition=%wide.while_cond.8, body=%wide.while_body.8.sunk | while | flops 2 | bytes 4195401 | solution.py:59
  421.8 3.8 bitcast_dynamic-update-slice_fusion.44
  426.2 3.9 bitcast_dynamic-update-slice_fusion.44
  432.5 8.7 %while.21 = (s32[]{:T(128)}, bf16[512,2,2048]{2,0,1:T(8,128)(2,1)}, s32[2,1]{0,1:T(1,128)S(1)}, bf16[2,512,2048]{2,1,0:T(8,128)(2,1)}, s32[]{:T(128)}) while((s32[]{:T(128)}, bf16[512,2,2048]{2,0,1:T(8,128)(2,1)}, s32[2,1]{0,1:T(1,128)S(1)}, bf16[2,512,2048]{2,1,0:T(8,128)(2,1)}, s32[]{:T(128)}) %tuple.213), condition=%wide.while_cond.9, body=%wide.while_body.9.sunk | while | flops 2 | bytes 4195401 | solution.py:59
  443.9 8.9 %while.22 = (s32[]{:T(128)}, bf16[512,2,2048]{2,0,1:T(8,128)(2,1)}, s32[2,1]{0,1:T(1,128)S(1)}, bf16[2,512,2048]{2,1,0:T(8,128)(2,1)}, s32[]{:T(128)}) while((s32[]{:T(128)}, bf16[512,2,2048]{2,0,1:T(8,128)(2,1)}, s32[2,1]{0,1:T(1,128)S(1)}, bf16[2,512,2048]{2,1,0:T(8,128)(2,1)}, s32[]{:T(128)}) %tuple.214), condition=%wide.while_cond.10, body=%wide.while_body.10.sunk | while | flops 2 | bytes 4195401 | solution.py:59
  444.5 3.9 bitcast_dynamic-update-slice_fusion.46
  448.9 3.9 bitcast_dynamic-update-slice_fusion.46
  455.3 9.4 %while.23 = (s32[]{:T(128)}, bf16[512,2,2048]{2,0,1:T(8,128)(2,1)}, s32[2,1]{0,1:T(1,128)S(1)}, bf16[2,512,2048]{2,1,0:T(8,128)(2,1)}, s32[]{:T(128)}) while((s32[]{:T(128)}, bf16[512,2,2048]{2,0,1:T(8,128)(2,1)}, s32[2,1]{0,1:T(1,128)S(1)}, bf16[2,512,2048]{2,1,0:T(8,128)(2,1)}, s32[]{:T(128)}) %tuple.215), condition=%wide.while_cond.11, body=%wide.while_body.11.sunk | while | flops 2 | bytes 4195401 | solution.py:59
  455.9 4.1 bitcast_dynamic-update-slice_fusion.47
  460.6 4.2 bitcast_dynamic-update-slice_fusion.47
  464.7 5.3 bitcast_dynamic-update-slice_fusion.23
  510.1 25.9 %fusion.1 = f32[2,6144,128]{1,2,0:T(8,128)} fusion(bf16[2,128,2048]{2,1,0:T(8,128)(2,1)S(1)} %bitcast.149, bf16[6144,2,2048]{2,0,1:T(8,128)(2,1)} %bitcast_dynamic-update-slice_fusion.12, pred[2]{0:T(512)(128)(4,1)S(1)} %maximum_compare_fusion), kind=kOutput, calls=%fused_computation.33 | convolution fusion | flops 6467616768 | bytes 57671680 | tf_op jit(solution)/shard_map/bri,dbi->brd/dot_general | solution.py:60
  536.0 10.6 %gather_fusion = f32[256,6144]{1,0:T(8,128)} fusion(f32[256,6144]{1,0:T(8,128)} %bitcast.147, s32[1024]{0:T(1024)S(1)} %copy-done.14), kind=kCustom, calls=%fused_computation | custom fusion | bytes 12583936 | tf_op jit(solution)/shard_map/gather | solution.py:66
  546.6 8.4 %reshape.505 = f32[128,2,6144]{2,1,0:T(2,128)} reshape(f32[256,6144]{1,0:T(8,128)} %gather_fusion) | data formatting | bytes 12582912 | tf_op jit(solution)/shard_map/gather | solution.py:66
  555.0 20.2 %fusion = f32[2,128,2048]{2,1,0:T(8,128)} fusion(bf16[6144,2,2048]{2,0,1:T(8,128)(2,1)} %bitcast_dynamic-update-slice_fusion.12, pred[2]{0:T(512)(128)(4,1)S(1)} %maximum_compare_fusion, bf16[2,128,6144]{2,1,0:T(8,128)(2,1)S(1)} %bitcast.148, pred[2,128]{1,0:T(4,128)(4,1)S(1)} %copy-done.22), kind=kOutput, calls=%fused_computation.32 | convolution fusion | flops 6469189632 | bytes 55574784 | tf_op jit(solution)/shard_map/brd,dbi->bri/dot_general | solution.py:63
  581.0 11.9 %multiply_reduce_fusion = bf16[128,6144]{1,0:T(8,128)(2,1)} fusion(f32[128,2,6144]{2,1,0:T(2,128)} %reshape.505, f32[128,2]{1,0:T(8,128)S(1)} %copy.20), kind=kLoop, calls=%fused_computation.35 | loop fusion | flops 2359296 | bytes 7865344 | tf_op jit(solution)/shard_map/reduce_sum | solution.py:66
  592.9 12.6 %copy.30 = bf16[768,2,2048]{2,1,0:T(2,128)(2,1)} copy(bf16[768,2,2048]{2,0,1:T(8,128)(2,1)} %reduce-scatter.5.cloned.1.call-done) | data formatting | bytes 12582912
  605.5 12.9 %psum.7 = f32[128,2]{0,1:T(2,128)} all-reduce(f32[128,2]{0,1:T(2,128)S(1)} %get-tuple-element.225), channel_id=1, replica_groups=mesh['fsdp'=8,'ep'=4] {'ep'}, use_global_device_ids=true, to_apply=%region_14.15 | all-reduce | flops 256 | bytes 2048 | tf_op jit(solution)/shard_map/psum | solution.py:82
  618.5 10.2 %reduce-scatter.3.cloned.1.call-done = bf16[128,1536]{1,0:T(8,128)(2,1)} async-done(((bf16[128,6144]{1,0:T(8,128)(2,1)}), bf16[128,1536]{1,0:T(8,128)(2,1)}) %reduce-scatter.3.cloned.1.call-update) | async-done | bytes 393232 | tf_op jit(solution)/shard_map/reduce_scatter | solution.py:77
  (146 shorter events, 112.0 us)
Async XLA Ops:
  7.2 42.2 %all-gather.5.cloned.1.call-start = ((), (), s32[]{:S(2)}) async-start(), calls=%async_computation.4 | async-start | bytes 1966080 | tf_op jit(solution)/shard_map/all_gather | solution.py:46
  7.9 274.8 %all-gather.3.cloned.1.call-start = ((), (), s32[]{:S(2)}) async-start(), calls=%async_computation.2 | async-start | bytes 56623104 | tf_op jit(solution)/shard_map/all_gather | solution.py:57
  16.3 0.7 copy-start.21
  16.3 4.7 copy-start.19
  16.4 576.5 %reduce-scatter.5.cloned.1.call-start = ((), (), s32[]{:S(2)}) async-start(), calls=%async_computation.5 | async-start | bytes 56623104 | tf_op jit(solution)/shard_map/reduce_scatter | solution.py:69
  17.1 6.4 %copy-start.17 = (s32[128,2]{0,1:T(2,128)}, s32[128,2]{0,1:T(2,128)S(1)}, u32[]{:S(2)}) copy-start(s32[128,2]{0,1:T(2,128)S(1)} %get-tuple-element.112) | copy-start | bytes 3076
  23.2 33.3 %copy-start.15 = (f32[256]{0:T(256)}, f32[256]{0:T(256)S(1)}, u32[]{:S(2)}) copy-start(f32[256]{0:T(256)S(1)} %scatter_custom_fusion) | copy-start | bytes 3076
  56.5 25.0 %copy-start.11 = (bf16[256,6144]{1,0:T(8,128)(2,1)}, bf16[256,6144]{1,0:T(8,128)(2,1)S(1)}, u32[]{:S(2)}) copy-start(bf16[256,6144]{1,0:T(8,128)(2,1)S(1)} %gather_fusion.1) | copy-start | bytes 9437188
  81.5 547.2 %reduce-scatter.3.cloned.1.call-start = ((), (), s32[]{:S(2)}) async-start(), calls=%async_computation.3 | async-start | bytes 1966080 | tf_op jit(solution)/shard_map/reduce_scatter | solution.py:77
  464.7 5.3 copy-start.1
  470.0 3.8 copy-start.2
  473.9 3.9 copy-start.3
  477.7 3.9 copy-start.4
  481.6 3.7 copy-start.5
  485.3 3.7 copy-start.6
  489.0 3.7 copy-start.7
  492.8 3.7 copy-start.8
  496.5 3.7 copy-start.9
  500.2 4.0 copy-start.10
  504.2 3.7 copy-start
  507.9 2.2 copy-start.13
  510.1 25.9 %copy-start.14 = (s32[1024]{0:T(1024)S(1)}, s32[1024]{0:T(1024)}, u32[]{:S(2)}) copy-start(s32[1024]{0:T(1024)} %pad_clamp_fusion.1) | copy-start | bytes 12292
  546.6 8.4 %copy-start.12 = (bf16[256,6144]{1,0:T(8,128)(2,1)S(1)}, bf16[256,6144]{1,0:T(8,128)(2,1)}, u32[]{:S(2)}) copy-start(bf16[256,6144]{1,0:T(8,128)(2,1)} %copy-done.11) | copy-start | bytes 9437188
  546.6 8.4 %copy-start.22 = (pred[2,128]{1,0:T(4,128)(4,1)S(1)}, pred[2,128]{1,0:T(4,128)(4,1)}, u32[]{:S(2)}) copy-start(pred[2,128]{1,0:T(4,128)(4,1)} %fusion.30) | copy-start | bytes 772
  555.0 20.2 %copy-start.16 = (f32[256]{0:T(256)S(1)}, f32[256]{0:T(256)}, u32[]{:S(2)}) copy-start(f32[256]{0:T(256)} %copy-done.15) | copy-start | bytes 3076
  578.4 2.4 copy-start.18
  578.4 2.4 copy-start.20
Sparse Core Ops, SparseCore 0:
  9.6 39.7 all-gather.4
  51.9 230.7 all-gather.2
  286.3 285.8 reduce-scatter.4
  593.0 35.6 reduce-scatter.2
where the time goes:
time: 642 us; the launch traced here: 635 us
  local copies, waits for them, and re-layouts  283 us (44%)
  waiting for transfers between devices  236 us (37%)
  matrix products  71.1 us (11%)
  other arithmetic  17 us (3%)
  between operations  14.3 us (2%)
  blocking collectives  12.9 us (2%)
    all_gather x1, waiting for transfers between devices, local(): piece = lax.all_gather(w_down, 'fsdp', axis=0, tiled=True)  200 us
    gather x48, local copies, waits for them, and re-layouts  109 us
    unnamed x73, local copies, waits for them, and re-layouts  98.7 us
    gather x1, local copies, waits for them, and re-layouts, local(): chosen = jnp.take(piece, safe_exp, axis=1)  41.5 us
    dot_general x1, matrix products, local(): jnp.einsum('bri,dbi->brd', hid_blocks, chosen, preferred_element_type=jnp...  25.9 us
    all_gather x1, waiting for transfers between devices, local(): full_grads = lax.all_gather(grad_out, 'ep', axis=1, tiled=True)  25.9 us
    dot_general x1, matrix products, local(): jnp.einsum('rd,rei->dei', scaled, masked_hid, preferred_element_type=jnp....  24.9 us
    dot_general x1, matrix products, local(): jnp.einsum('brd,dbi->bri', routed_blocks, chosen, preferred_element_type=...  20.2 us
  transfers between devices with their start and end apart: 4, of which 3 were waited for; matrix products, arithmetic and copies ran while one was open for 56% of the time, Pallas kernels for 0%

commit v1 on v0

--- a/solution.py
+++ b/solution.py
@@ -4,6 +4,24 @@
 from jax.sharding import PartitionSpec as P
 
 BLOCK = 128
+
+
+def laid_out(blocks, dim):
+    shape = list(blocks.shape[1:])
+    shape[dim] *= blocks.shape[0]
+    return jnp.moveaxis(blocks, 0, dim).reshape(shape)
+
+
+def doubled(x, axis):
+    peers = lax.axis_size(axis)
+    blocks = x[None]
+    for level in range(peers.bit_length() - 1):
+        bit = 1 << level
+        other = lax.ppermute(blocks, axis, [(i, i ^ bit) for i in range(peers)])
+        both = jnp.stack([blocks, other])
+        upper = lax.axis_index(axis) >> level & 1
+        blocks = jnp.where(upper == 0, both, both[::-1]).reshape(-1, *x.shape)
+    return blocks
 
 
 def route_layout(route_part, prob_part, expert_count, block_rows, row_count):
@@ -43,7 +61,7 @@
     )
     safe_exp = jnp.maximum(block_exp, 0)
     prob_valid = probs * valid.astype(jnp.float32)
-    full_grads = lax.all_gather(grad_out, "ep", axis=1, tiled=True)
+    full_grads = laid_out(doubled(grad_out, "ep"), 1)
     model_width = full_grads.shape[1]
     routed = jnp.where(row_live[:, None] > 0, full_grads[row_tok], jnp.zeros((), jnp.bfloat16))
     scaled = (row_prob[:, None] * routed.astype(jnp.float32)).astype(jnp.bfloat16)

time: 642 us -> 613 us (0.955)
  waiting for transfers between devices: 236 us -> 202 us
    all_gather x1, waiting for transfers between devices: 200 us -> 156 us  [local(): piece = lax.all_gather(w_down, 'fsdp', axis=0, tiled=True)]
    ppermute x0 -> x2, waiting for transfers between devices: none -> 35.5 us  [doubled(): other = lax.ppermute(blocks, axis, [(i, i ^ bit) for i in range(peers)])]
    all_gather x1 -> x0, waiting for transfers between devices: 25.9 us -> none  [local(): full_grads = lax.all_gather(grad_out, 'ep', axis=1, tiled=True)]
    unnamed x73 -> x74, local copies, waits for them, and re-layouts: 98.7 us -> 101 us
  transfers between devices with their start and end apart: 4 -> 5, of which waited for: 3 -> 4; matrix products, arithmetic and copies ran while one was open for 56% -> 57% of each run, Pallas kernels for 0% -> 0%
where the time goes in v1:
time: 613 us; the launch traced here: 605 us
  local copies, waits for them, and re-layouts  283 us (46%)
  waiting for transfers between devices  202 us (33%)
  matrix products  69.5 us (11%)
  other arithmetic  17.1 us (3%)
  between operations  14.3 us (2%)
  blocking collectives  12.8 us (2%)
  starting transfers between devices  6.14 us (1%)
    all_gather x1, waiting for transfers between devices, local(): piece = lax.all_gather(w_down, 'fsdp', axis=0, tiled=True)  156 us
    gather x48, local copies, waits for them, and re-layouts  109 us
    unnamed x74, local copies, waits for them, and re-layouts  101 us
    gather x1, local copies, waits for them, and re-layouts, local(): chosen = jnp.take(piece, safe_exp, axis=1)  41.5 us
    ppermute x2, waiting for transfers between devices, doubled(): other = lax.ppermute(blocks, axis, [(i, i ^ bit) for i in range(peers)])  35.5 us
    dot_general x1, matrix products, local(): jnp.einsum('bri,dbi->brd', hid_blocks, chosen, preferred_element_type=jnp...  25.5 us
    dot_general x1, matrix products, local(): jnp.einsum('rd,rei->dei', scaled, masked_hid, preferred_element_type=jnp....  22.6 us
    dot_general x1, matrix products, local(): jnp.einsum('brd,dbi->bri', routed_blocks, chosen, preferred_element_type=...  21.3 us
  transfers between devices with their start and end apart: 5, of which 4 were waited for; matrix products, arithmetic and copies ran while one was open for 57% of the time, Pallas kernels for 0%

profile of v1, /device:TPU:0, one launch (start us, length us, event | category | flops | bytes accessed | tf_op | source)
XLA Modules:
  0.0 605.4 jit_solution(18287039363259036152)
XLA Ops:
  7.2 8.4 %copy.23 = bf16[768,2,2048]{2,0,1:T(8,128)(2,1)} copy(bf16[768,2,2048]{2,1,0:T(2,128)(2,1)} %param.6) | data formatting | bytes 12582912 | tf_op args[1]
  22.4 6.3 %collective-permute-done = bf16[1,128,1536]{2,1,0:T(8,128)(2,1)S(1)} collective-permute-done((bf16[1,128,1536]{2,1,0:T(8,128)(2,1)S(1)}, bf16[1,128,1536]{2,1,0:T(8,128)(2,1)S(1)}, u32[]{:S(2)}, u32[]{:S(2)}) %collective-permute-start) | collective-permute-done | bytes 393248 | tf_op jit(solution)/shard_map/ppermute | solution.py:20
  36.4 29.2 %collective-permute-done.1 = bf16[2,128,1536]{2,1,0:T(8,128)(2,1)S(1)} collective-permute-done((bf16[2,128,1536]{2,1,0:T(8,128)(2,1)S(1)}, bf16[2,128,1536]{2,1,0:T(8,128)(2,1)S(1)}, u32[]{:S(2)}, u32[]{:S(2)}) %collective-permute-start.1) | collective-permute-done | bytes 786464 | tf_op jit(solution)/shard_map/ppermute | solution.py:20
  67.5 4.2 gather_fusion.1
  71.7 22.6 %convolution_convert_fusion = bf16[6144,2,2048]{2,0,1:T(8,128)(2,1)} fusion(bf16[256,6144]{1,0:T(8,128)(2,1)} %gather_fusion.1, f32[256]{0:T(256)S(1)} %scatter_custom_fusion, pred[256]{0:T(512)(128)(4,1)S(1)} %broadcast_compare_fusion, bf16[256,2]{0,1:T(2,128)(2,1)S(1)} %compare_convert_fusion, bf16[256,2048]{1,0:T(8,128)(2,1)S(1)} %copy-done.12), kind=kOutput, calls=%fused_computation.31 | convolution fusion | flops 12920553472 | bytes 54528256 | tf_op jit(solution)/shard_map/rd,rei->dei/dot_general | solution.py:88
  94.5 155.8 %all-gather.2.cloned.1.call-done = bf16[6144,2,2048]{2,0,1:T(8,128)(2,1)} async-done(((bf16[768,2,2048]{2,0,1:T(8,128)(2,1)}), bf16[6144,2,2048]{2,0,1:T(8,128)(2,1)}) %all-gather.2.cloned.1.call-update) | async-done | bytes 50331664 | tf_op jit(solution)/shard_map/all_gather | solution.py:75
  250.3 41.5 %fusion.30 = (bf16[512,2,2048]{2,0,1:T(8,128)(2,1)}, bf16[512,2,2048]{2,0,1:T(8,128)(2,1)}, bf16[512,2,2048]{2,0,1:T(8,128)(2,1)}, bf16[512,2,2048]{2,0,1:T(8,12...) fusion(bf16[6144,2,2048]{2,0,1:T(8,128)(2,1)} %all-gather.2.clo, ...), kind=kLoop, calls=%fused_computation.114 | loop fusion | bytes 100663296 | tf_op jit(solution)/shard_map/jit(_take)/gather | solution.py:77
  294.9 9.6 %while.12 = (s32[]{:T(128)}, bf16[512,2,2048]{2,0,1:T(8,128)(2,1)}, s32[2,1]{0,1:T(1,128)S(1)}, bf16[2,512,2048]{2,1,0:T(8,128)(2,1)}, s32[]{:T(128)}) while((s32[]{:T(128)}, bf16[512,2,2048]{2,0,1:T(8,128)(2,1)}, s32[2,1]{0,1:T(1,128)S(1)}, bf16[2,512,2048]{2,1,0:T(8,128)(2,1)}, s32[]{:T(128)}) %tuple.163), condition=%wide.while_cond, body=%wide.while_body.sunk | while | flops 2 | bytes 4195401 | solution.py:77
  295.5 4.2 bitcast_dynamic-update-slice_fusion.36
  300.3 4.2 bitcast_dynamic-update-slice_fusion.36
  307.6 9.4 %while.13 = (s32[]{:T(128)}, bf16[512,2,2048]{2,0,1:T(8,128)(2,1)}, s32[2,1]{0,1:T(1,128)S(1)}, bf16[2,512,2048]{2,1,0:T(8,128)(2,1)}, s32[]{:T(128)}) while((s32[]{:T(128)}, bf16[512,2,2048]{2,0,1:T(8,128)(2,1)}, s32[2,1]{0,1:T(1,128)S(1)}, bf16[2,512,2048]{2,1,0:T(8,128)(2,1)}, s32[]{:T(128)}) %tuple.205), condition=%wide.while_cond.1, body=%wide.while_body.1.sunk | while | flops 2 | bytes 4195401 | solution.py:77
  308.2 4.3 bitcast_dynamic-update-slice_fusion.37
  313.1 4.0 bitcast_dynamic-update-slice_fusion.37
  319.6 8.9 %while.14 = (s32[]{:T(128)}, bf16[512,2,2048]{2,0,1:T(8,128)(2,1)}, s32[2,1]{0,1:T(1,128)S(1)}, bf16[2,512,2048]{2,1,0:T(8,128)(2,1)}, s32[]{:T(128)}) while((s32[]{:T(128)}, bf16[512,2,2048]{2,0,1:T(8,128)(2,1)}, s32[2,1]{0,1:T(1,128)S(1)}, bf16[2,512,2048]{2,1,0:T(8,128)(2,1)}, s32[]{:T(128)}) %tuple.206), condition=%wide.while_cond.2, body=%wide.while_body.2.sunk | while | flops 2 | bytes 4195401 | solution.py:77
  320.2 3.8 bitcast_dynamic-update-slice_fusion.38
  324.6 3.9 bitcast_dynamic-update-slice_fusion.38
  331.0 9.2 %while.15 = (s32[]{:T(128)}, bf16[512,2,2048]{2,0,1:T(8,128)(2,1)}, s32[2,1]{0,1:T(1,128)S(1)}, bf16[2,512,2048]{2,1,0:T(8,128)(2,1)}, s32[]{:T(128)}) while((s32[]{:T(128)}, bf16[512,2,2048]{2,0,1:T(8,128)(2,1)}, s32[2,1]{0,1:T(1,128)S(1)}, bf16[2,512,2048]{2,1,0:T(8,128)(2,1)}, s32[]{:T(128)}) %tuple.207), condition=%wide.while_cond.3, body=%wide.while_body.3.sunk | while | flops 2 | bytes 4195401 | solution.py:77
  331.6 4.1 bitcast_dynamic-update-slice_fusion.39
  336.3 3.9 bitcast_dynamic-update-slice_fusion.39
  342.8 9.1 %while.16 = (s32[]{:T(128)}, bf16[512,2,2048]{2,0,1:T(8,128)(2,1)}, s32[2,1]{0,1:T(1,128)S(1)}, bf16[2,512,2048]{2,1,0:T(8,128)(2,1)}, s32[]{:T(128)}) while((s32[]{:T(128)}, bf16[512,2,2048]{2,0,1:T(8,128)(2,1)}, s32[2,1]{0,1:T(1,128)S(1)}, bf16[2,512,2048]{2,1,0:T(8,128)(2,1)}, s32[]{:T(128)}) %tuple.208), condition=%wide.while_cond.4, body=%wide.while_body.4.sunk | while | flops 2 | bytes 4195401 | solution.py:77
  343.3 3.9 bitcast_dynamic-update-slice_fusion.40
  347.8 4.1 bitcast_dynamic-update-slice_fusion.40
  354.4 8.8 %while.17 = (s32[]{:T(128)}, bf16[512,2,2048]{2,0,1:T(8,128)(2,1)}, s32[2,1]{0,1:T(1,128)S(1)}, bf16[2,512,2048]{2,1,0:T(8,128)(2,1)}, s32[]{:T(128)}) while((s32[]{:T(128)}, bf16[512,2,2048]{2,0,1:T(8,128)(2,1)}, s32[2,1]{0,1:T(1,128)S(1)}, bf16[2,512,2048]{2,1,0:T(8,128)(2,1)}, s32[]{:T(128)}) %tuple.209), condition=%wide.while_cond.5, body=%wide.while_body.5.sunk | while | flops 2 | bytes 4195401 | solution.py:77
  359.3 3.8 bitcast_dynamic-update-slice_fusion.41
  365.7 8.8 %while.18 = (s32[]{:T(128)}, bf16[512,2,2048]{2,0,1:T(8,128)(2,1)}, s32[2,1]{0,1:T(1,128)S(1)}, bf16[2,512,2048]{2,1,0:T(8,128)(2,1)}, s32[]{:T(128)}) while((s32[]{:T(128)}, bf16[512,2,2048]{2,0,1:T(8,128)(2,1)}, s32[2,1]{0,1:T(1,128)S(1)}, bf16[2,512,2048]{2,1,0:T(8,128)(2,1)}, s32[]{:T(128)}) %tuple.210), condition=%wide.while_cond.6, body=%wide.while_body.6.sunk | while | flops 2 | bytes 4195401 | solution.py:77
  366.3 3.8 bitcast_dynamic-update-slice_fusion.42
  370.7 3.9 bitcast_dynamic-update-slice_fusion.42
  377.1 9.3 %while.19 = (s32[]{:T(128)}, bf16[512,2,2048]{2,0,1:T(8,128)(2,1)}, s32[2,1]{0,1:T(1,128)S(1)}, bf16[2,512,2048]{2,1,0:T(8,128)(2,1)}, s32[]{:T(128)}) while((s32[]{:T(128)}, bf16[512,2,2048]{2,0,1:T(8,128)(2,1)}, s32[2,1]{0,1:T(1,128)S(1)}, bf16[2,512,2048]{2,1,0:T(8,128)(2,1)}, s32[]{:T(128)}) %tuple.211), condition=%wide.while_cond.7, body=%wide.while_body.7.sunk | while | flops 2 | bytes 4195401 | solution.py:77
  377.7 4.2 bitcast_dynamic-update-slice_fusion.43
  382.4 4.0 bitcast_dynamic-update-slice_fusion.43
  388.9 8.8 %while.20 = (s32[]{:T(128)}, bf16[512,2,2048]{2,0,1:T(8,128)(2,1)}, s32[2,1]{0,1:T(1,128)S(1)}, bf16[2,512,2048]{2,1,0:T(8,128)(2,1)}, s32[]{:T(128)}) while((s32[]{:T(128)}, bf16[512,2,2048]{2,0,1:T(8,128)(2,1)}, s32[2,1]{0,1:T(1,128)S(1)}, bf16[2,512,2048]{2,1,0:T(8,128)(2,1)}, s32[]{:T(128)}) %tuple.212), condition=%wide.while_cond.8, body=%wide.while_body.8.sunk | while | flops 2 | bytes 4195401 | solution.py:77
  393.8 3.9 bitcast_dynamic-update-slice_fusion.44
  400.2 8.7 %while.21 = (s32[]{:T(128)}, bf16[512,2,2048]{2,0,1:T(8,128)(2,1)}, s32[2,1]{0,1:T(1,128)S(1)}, bf16[2,512,2048]{2,1,0:T(8,128)(2,1)}, s32[]{:T(128)}) while((s32[]{:T(128)}, bf16[512,2,2048]{2,0,1:T(8,128)(2,1)}, s32[2,1]{0,1:T(1,128)S(1)}, bf16[2,512,2048]{2,1,0:T(8,128)(2,1)}, s32[]{:T(128)}) %tuple.213), condition=%wide.while_cond.9, body=%wide.while_body.9.sunk | while | flops 2 | bytes 4195401 | solution.py:77
  411.5 9.0 %while.22 = (s32[]{:T(128)}, bf16[512,2,2048]{2,0,1:T(8,128)(2,1)}, s32[2,1]{0,1:T(1,128)S(1)}, bf16[2,512,2048]{2,1,0:T(8,128)(2,1)}, s32[]{:T(128)}) while((s32[]{:T(128)}, bf16[512,2,2048]{2,0,1:T(8,128)(2,1)}, s32[2,1]{0,1:T(1,128)S(1)}, bf16[2,512,2048]{2,1,0:T(8,128)(2,1)}, s32[]{:T(128)}) %tuple.214), condition=%wide.while_cond.10, body=%wide.while_body.10.sunk | while | flops 2 | bytes 4195401 | solution.py:77
  412.1 3.9 bitcast_dynamic-update-slice_fusion.46
  416.6 3.9 bitcast_dynamic-update-slice_fusion.46
  423.0 9.4 %while.23 = (s32[]{:T(128)}, bf16[512,2,2048]{2,0,1:T(8,128)(2,1)}, s32[2,1]{0,1:T(1,128)S(1)}, bf16[2,512,2048]{2,1,0:T(8,128)(2,1)}, s32[]{:T(128)}) while((s32[]{:T(128)}, bf16[512,2,2048]{2,0,1:T(8,128)(2,1)}, s32[2,1]{0,1:T(1,128)S(1)}, bf16[2,512,2048]{2,1,0:T(8,128)(2,1)}, s32[]{:T(128)}) %tuple.215), condition=%wide.while_cond.11, body=%wide.while_body.11.sunk | while | flops 2 | bytes 4195401 | solution.py:77
  423.6 4.1 bitcast_dynamic-update-slice_fusion.47
  428.2 4.2 bitcast_dynamic-update-slice_fusion.47
  432.4 5.3 bitcast_dynamic-update-slice_fusion.23
  479.0 21.3 %fusion = f32[2,128,2048]{2,1,0:T(8,128)} fusion(bf16[6144,2,2048]{2,0,1:T(8,128)(2,1)} %bitcast_dynamic-update-slice_fusion.12, pred[2]{0:T(512)(128)(4,1)S(1)} %maximum_compare_fusion, bf16[2,128,6144]{2,1,0:T(8,128)(2,1)S(1)} %bitcast.161, pred[2,128]{1,0:T(4,128)(4,1)S(1)} %fusion.32), kind=kOutput, calls=%fused_computation.32 | convolution fusion | flops 6469189632 | bytes 55574784 | tf_op jit(solution)/shard_map/brd,dbi->bri/dot_general | solution.py:81
  505.9 25.5 %fusion.1 = f32[2,6144,128]{1,2,0:T(8,128)} fusion(bf16[2,128,2048]{2,1,0:T(8,128)(2,1)S(1)} %bitcast.162, bf16[6144,2,2048]{2,0,1:T(8,128)(2,1)} %bitcast_dynamic-update-slice_fusion.12, pred[2]{0:T(512)(128)(4,1)S(1)} %maximum_compare_fusion), kind=kOutput, calls=%fused_computation.33 | convolution fusion | flops 6467616768 | bytes 57671680 | tf_op jit(solution)/shard_map/bri,dbi->brd/dot_general | solution.py:78
  531.4 10.6 %gather_fusion = f32[256,6144]{1,0:T(8,128)} fusion(f32[256,6144]{1,0:T(8,128)} %bitcast.160, s32[1024]{0:T(1024)S(1)} %copy-done.14), kind=kCustom, calls=%fused_computation | custom fusion | bytes 12583936 | tf_op jit(solution)/shard_map/gather | solution.py:84
  542.0 8.4 %reshape.517 = f32[128,2,6144]{2,1,0:T(2,128)} reshape(f32[256,6144]{1,0:T(8,128)} %gather_fusion) | data formatting | bytes 12582912 | tf_op jit(solution)/shard_map/gather | solution.py:84
  550.4 11.9 %multiply_reduce_fusion = bf16[128,6144]{1,0:T(8,128)(2,1)} fusion(f32[128,2,6144]{2,1,0:T(2,128)} %reshape.517, f32[128,2]{1,0:T(8,128)S(1)} %copy.22), kind=kLoop, calls=%fused_computation.35 | loop fusion | flops 2359296 | bytes 7865344 | tf_op jit(solution)/shard_map/reduce_sum | solution.py:84
  562.3 12.6 %copy.33 = bf16[768,2,2048]{2,1,0:T(2,128)(2,1)} copy(bf16[768,2,2048]{2,0,1:T(8,128)(2,1)} %reduce-scatter.5.cloned.1.call-done) | data formatting | bytes 12582912
  574.9 12.8 %psum.7 = f32[128,2]{0,1:T(2,128)} all-reduce(f32[128,2]{0,1:T(2,128)S(1)} %get-tuple-element.227), channel_id=1, replica_groups=mesh['fsdp'=8,'ep'=4] {'ep'}, use_global_device_ids=true, to_apply=%region_14.15 | all-reduce | flops 256 | bytes 2048 | tf_op jit(solution)/shard_map/psum | solution.py:100
  587.7 10.9 %reduce-scatter.3.cloned.1.call-done = bf16[128,1536]{1,0:T(8,128)(2,1)} async-done(((bf16[128,6144]{1,0:T(8,128)(2,1)}), bf16[128,1536]{1,0:T(8,128)(2,1)}) %reduce-scatter.3.cloned.1.call-update) | async-done | bytes 393232 | tf_op jit(solution)/shard_map/reduce_scatter | solution.py:95
  (152 shorter events, 124.0 us)
Async XLA Ops:
  7.2 243.2 %all-gather.2.cloned.1.call-start = ((), (), s32[]{:S(2)}) async-start(), calls=%async_computation.2 | async-start | bytes 56623104 | tf_op jit(solution)/shard_map/all_gather | solution.py:75
  15.6 1.0 copy-start.15
  15.6 4.0 copy-start.22
  15.6 17.9 %copy-start.20 = (f32[128,2]{0,1:T(2,128)S(1)}, f32[128,2]{0,1:T(2,128)}, u32[]{:S(2)}) copy-start(f32[128,2]{0,1:T(2,128)} %param.8) | copy-start | bytes 3076
  15.6 546.7 %reduce-scatter.5.cloned.1.call-start = ((), (), s32[]{:S(2)}) async-start(), calls=%async_computation.4 | async-start | bytes 56623104 | tf_op jit(solution)/shard_map/reduce_scatter | solution.py:87
  16.6 12.1 %collective-permute-start = (bf16[1,128,1536]{2,1,0:T(8,128)(2,1)S(1)}, bf16[1,128,1536]{2,1,0:T(8,128)(2,1)S(1)}, u32[]{:S(2)}, u32[]{:S(2)}) collective-permute-start(bf16[1,128,1536]{2,1,0:T(8,128)(2,1)S(1)} %bitcast.166), channel_id=1, source_target_pairs={{0,1},{1,0},{2,3},{3,2},{4,5},{5,4},{6,7},{7,6},{8,9},{9,8},{10,11... | collective-permute-start | bytes 1179656 | tf_op jit(solution)/shard_map/ppermute | solution.py:20
  19.7 9.0 %copy-start.18 = (s32[128,2]{0,1:T(2,128)}, s32[128,2]{0,1:T(2,128)S(1)}, u32[]{:S(2)}) copy-start(s32[128,2]{0,1:T(2,128)S(1)} %get-tuple-element.112) | copy-start | bytes 3076
  29.0 36.5 %collective-permute-start.1 = (bf16[2,128,1536]{2,1,0:T(8,128)(2,1)S(1)}, bf16[2,128,1536]{2,1,0:T(8,128)(2,1)S(1)}, u32[]{:S(2)}, u32[]{:S(2)}) collective-permute-start(bf16[2,128,1536]{2,1,0:T(8,128)(2,1)S(1)} %get-tuple-element.226), channel_id=1, source_target_pairs={{0,2},{1,3},{2,0},{3,1},{4,6},{5,7},{6,4},{7,5},{8,10},{9,11},{10,... | collective-permute-start | bytes 2359304 | tf_op jit(solution)/shard_map/ppermute | solution.py:20
  35.7 36.0 %copy-start.16 = (f32[256]{0:T(256)}, f32[256]{0:T(256)S(1)}, u32[]{:S(2)}) copy-start(f32[256]{0:T(256)S(1)} %scatter_custom_fusion) | copy-start | bytes 3076
  67.5 4.2 copy-start.12
  94.3 504.3 %reduce-scatter.3.cloned.1.call-start = ((), (), s32[]{:S(2)}) async-start(), calls=%async_computation.3 | async-start | bytes 1966080 | tf_op jit(solution)/shard_map/reduce_scatter | solution.py:95
  432.4 5.3 copy-start.1
  437.6 3.8 copy-start.2
  441.5 3.9 copy-start.3
  445.4 3.8 copy-start.4
  449.2 3.7 copy-start.5
  452.9 3.7 copy-start.6
  456.6 3.7 copy-start.7
  460.4 3.7 copy-start.8
  464.1 3.7 copy-start.9
  467.8 4.0 copy-start.10
  471.8 3.7 copy-start
  475.5 3.5 copy-start.11
  479.0 21.3 %copy-start.17 = (f32[256]{0:T(256)S(1)}, f32[256]{0:T(256)}, u32[]{:S(2)}) copy-start(f32[256]{0:T(256)} %copy-done.16) | copy-start | bytes 3076
  500.3 3.2 copy-start.14
  503.5 2.2 copy-start.19
  503.5 2.2 copy-start.21
  503.6 2.3 copy-start.13
Sparse Core Ops, SparseCore 0:
  15.7 234.5 all-gather.1
  254.0 285.8 reduce-scatter.4
  562.4 36.1 reduce-scatter.2
